TPU v7x, 32 devices: a whole 2x2x4 slice. The times are simulated.
32 devices in a mesh: fsdp: 2 (over y), ctx: 4 (over z), tp: 4 (over x, core).
Axes of the slice: x: 2, y: 2, z: 4, core: 2. Of those that a mesh axis runs over, the one named last changes fastest.
Arguments:
- tokens: bfloat16 [4, 4, 1024, 1024], P(None, 'fsdp', 'ctx', 'tp'), may hold values from -6 to 6
- skip_tokens: bfloat16 [4, 4, 1024, 1024], P(None, 'fsdp', 'ctx', 'tp'), may hold values from -6 to 6
- merger_weight: bfloat16 [1024, 2, 1024], P(('fsdp', 'ctx'), None, 'tp'), may hold values from -0.125 to 0.125
- merger_bias: float32 [1024], P(('fsdp', 'ctx', 'tp')), may hold values from -3 to 3
- first_gain: float32 [1024], P(('fsdp', 'ctx', 'tp')), may hold values from 0.25 to 1.75
- first_shift: float32 [1024], P(('fsdp', 'ctx', 'tp')), may hold values from -2 to 2
- attend_weight: bfloat16 [1024, 3, 1024], P(('fsdp', 'ctx'), None, 'tp'), may hold values from -0.25 to 0.25
- output_weight: bfloat16 [1024, 1024], P(('fsdp', 'ctx'), 'tp'), may hold values from -0.75 to 0.75
- output_bias: float32 [1024], P(('fsdp', 'ctx', 'tp')), may hold values from -2 to 2
- second_gain: float32 [1024], P(('fsdp', 'ctx', 'tp')), may hold values from 0.25 to 1.75
- second_shift: float32 [1024], P(('fsdp', 'ctx', 'tp')), may hold values from -2 to 2
- expand_weight: bfloat16 [1024, 4096], P(('fsdp', 'ctx'), 'tp'), may hold values from -0.1875 to 0.1875
- widen_bias: float32 [4096], P(('fsdp', 'ctx', 'tp')), may hold values from -3 to 3
- shrink_weight: bfloat16 [1024, 4096], P(('fsdp', 'ctx'), 'tp'), may hold values from -0.125 to 0.125
- shrink_bias: float32 [1024], P(('fsdp', 'ctx', 'tp')), may hold values from -2 to 2
- live_slots: int32 [4, 4], P(None, 'fsdp'), may hold values from 0 to 1, as said below
- cotangent: bfloat16 [4, 4, 1024, 1024], P(None, 'fsdp', ('ctx', 'tp')), may hold values from -6 to 6
Outputs:
- layer_out: bfloat16 [4, 4, 1024, 1024], P(None, 'fsdp', ('ctx', 'tp'))
- grad_tokens: float32 [4, 4, 1024, 1024], P(None, 'fsdp', 'ctx', 'tp')
- grad_skip: float32 [4, 4, 1024, 1024], P(None, 'fsdp', 'ctx', 'tp')
- weight_merger: float32 [1024, 2, 1024], P(('fsdp', 'ctx'), None, 'tp')
- bias_merger: float32 [1024], P(('fsdp', 'ctx', 'tp'))
- gain_first: float32 [1024], P(('fsdp', 'ctx', 'tp'))
- shift_first: float32 [1024], P(('fsdp', 'ctx', 'tp'))
- weight_attend: float32 [1024, 3, 1024], P(('fsdp', 'ctx'), None, 'tp')
- weight_output: float32 [1024, 1024], P(('fsdp', 'ctx'), 'tp')
- bias_output: float32 [1024], P(('fsdp', 'ctx', 'tp'))
- gain_second: float32 [1024], P(('fsdp', 'ctx', 'tp'))
- shift_second: float32 [1024], P(('fsdp', 'ctx', 'tp'))
- weight_expand: float32 [1024, 4096], P(('fsdp', 'ctx'), 'tp')
- bias_expand: float32 [4096], P(('fsdp', 'ctx', 'tp'))
- weight_shrink: float32 [1024, 4096], P(('fsdp', 'ctx'), 'tp')
- bias_shrink: float32 [1024], P(('fsdp', 'ctx', 'tp'))
Inputs may be any that keep to these rules, and one draw needn't show every extreme that they name: `live_slots`: in every micro-batch but the last exactly one of the 4 slots is empty (0), in the last exactly two; the empty slots lie anywhere.
All inputs are finite; a program needn't handle non-finite values.
Results may differ from a plain program's by a relative error of at most 0.017.
Values may be sent and summed in bfloat16 or wider, within the bound.
No kernel may reach another device: no remote copies, remote signals or barrier semaphores. Data moves between devices by JAX's collectives and lax.ppermute only.
A program may use at most 256 MiB of HBM per device.

v0:
```python
import jax
import jax.numpy as jnp
from jax import lax
from jax.sharding import PartitionSpec as P

HD = 64
EPSILON = 1e-05


def layer_norm(matrix, scales, shifts):
    center = matrix - jnp.mean(matrix, axis=-1, keepdims=True)
    spread = jnp.mean(center * center, axis=-1, keepdims=True)
    return center * lax.rsqrt(spread + EPSILON) * scales + shifts


def gelu_exact(matrix):
    return jax.nn.gelu(matrix, approximate=False)


def fetch(merger_part, attend_part, output_part, expand_part, shrink_part):
    return (
        lax.all_gather(merger_part, ("fsdp", "ctx"), axis=0, tiled=True),
        lax.all_gather(attend_part, ("fsdp", "ctx"), axis=0, tiled=True),
        lax.all_gather(output_part, ("fsdp", "ctx"), axis=0, tiled=True),
        lax.all_gather(expand_part, ("fsdp", "ctx"), axis=0, tiled=True),
        lax.all_gather(shrink_part, ("fsdp", "ctx"), axis=0, tiled=True),
    )


def spread_rows(block):
    return lax.all_gather(block, "tp", axis=1, tiled=True)


def fold_rows(block):
    return lax.psum_scatter(block, "tp", scatter_dimension=1, tiled=True)


def reduce_weights(parts):
    return (
        lax.psum_scatter(parts[0], ("fsdp", "ctx"), scatter_dimension=0, tiled=True),
        lax.psum_scatter(parts[1], ("fsdp", "ctx"), scatter_dimension=0, tiled=True),
        lax.psum_scatter(parts[2], ("fsdp", "ctx"), scatter_dimension=0, tiled=True),
        lax.psum_scatter(parts[3], ("fsdp", "ctx"), scatter_dimension=0, tiled=True),
        lax.psum_scatter(parts[4], ("fsdp", "ctx"), scatter_dimension=0, tiled=True),
    )


def micro_step(weights, vectors, tokens_now, skips_now, live_now, cot_now, tensor_rank):
    merger_full, attend_full, output_full, expand_full, shrink_full = weights
    (
        merger_bias,
        first_gain,
        first_shift,
        output_bias,
        second_gain,
        second_shift,
        shrink_bias,
        widen_bias,
    ) = vectors
    groups = tokens_now.shape[0]
    local_len = tokens_now.shape[1]
    heads_dev = attend_full.shape[2] // HD
    hidden = expand_full.shape[1]
    scaling = HD ** (-0.5)
    stacked = jnp.stack([tokens_now, skips_now], axis=2)
    joined = (
        fold_rows(
            jnp.einsum("stci,oci->sto", stacked, merger_full, preferred_element_type=jnp.float32)
        )
        + merger_bias
    )
    normed, first_pull = jax.vjp(layer_norm, joined, first_gain, first_shift)
    normed_all = spread_rows(normed.astype(jnp.bfloat16))
    project = jnp.einsum(
        "std,dcj->stcj", normed_all, attend_full, preferred_element_type=jnp.float32
    ).astype(jnp.bfloat16)
    key_rows, value_rows = (
        lax.all_gather(project[:, :, 1], "ctx", axis=1, tiled=True),
        lax.all_gather(project[:, :, 2], "ctx", axis=1, tiled=True),
    )
    seq_len = key_rows.shape[1]
    query_heads = project[:, :, 0].reshape(groups, local_len, heads_dev, HD)
    key_heads = key_rows.reshape(groups, seq_len, heads_dev, HD)
    value_heads = value_rows.reshape(groups, seq_len, heads_dev, HD)
    scores = (
        jnp.einsum("sqhd,skhd->shqk", query_heads, key_heads, preferred_element_type=jnp.float32)
        * scaling
    )
    row_peak = jnp.max(scores, axis=-1, keepdims=True)
    logsum = row_peak + jnp.log(jnp.sum(jnp.exp(scores - row_peak), axis=-1, keepdims=True))
    probs_low = jnp.exp(scores - logsum).astype(jnp.bfloat16)
    attended = jnp.einsum(
        "shqk,skhd->sqhd", probs_low, value_heads, preferred_element_type=jnp.float32
    )
    attended = attended.astype(jnp.bfloat16).reshape(groups, local_len, heads_dev * HD)
    second = (
        joined
        + fold_rows(
            jnp.einsum("sti,oi->sto", attended, output_full, preferred_element_type=jnp.float32)
        )
        + output_bias
    )
    normed_two, second_pull = jax.vjp(layer_norm, second, second_gain, second_shift)
    normed_two_all = spread_rows(normed_two.astype(jnp.bfloat16))
    bias_slice = lax.dynamic_slice_in_dim(widen_bias, tensor_rank * hidden, hidden)
    widened_hidden = (
        jnp.einsum("std,df->stf", normed_two_all, expand_full, preferred_element_type=jnp.float32)
        + bias_slice
    )
    activated, gelu_pull = jax.vjp(gelu_exact, widened_hidden)
    activated_low = activated.astype(jnp.bfloat16)
    result = (
        second
        + fold_rows(
            jnp.einsum(
                "stf,of->sto", activated_low, shrink_full, preferred_element_type=jnp.float32
            )
        )
        + shrink_bias
    )
    live_mask = live_now.astype(jnp.float32)[:, None, None]
    layer_out = (result * live_mask).astype(jnp.bfloat16)
    upstream = cot_now.astype(jnp.float32) * live_mask
    grad_shrink_bias = jnp.sum(upstream, axis=(0, 1))
    branch_low = spread_rows(upstream.astype(jnp.bfloat16))
    grad_shrink = jnp.einsum(
        "sto,stf->of", branch_low, activated_low, preferred_element_type=jnp.float32
    )
    grad_activated = jnp.einsum(
        "sto,of->stf", branch_low, shrink_full, preferred_element_type=jnp.float32
    )
    grad_expanded = gelu_pull(grad_activated)[0].astype(jnp.bfloat16)
    grad_expand_bias = jnp.sum(grad_expanded, axis=(0, 1), dtype=jnp.float32)
    grad_expand = jnp.einsum(
        "std,stf->df", normed_two_all, grad_expanded, preferred_element_type=jnp.float32
    )
    grad_normed_two = fold_rows(
        jnp.einsum("stf,df->std", grad_expanded, expand_full, preferred_element_type=jnp.float32)
    )
    grad_second_norm, grad_second_gain, grad_second_shift = second_pull(grad_normed_two)
    grad_second = upstream + grad_second_norm
    grad_output_bias = jnp.sum(grad_second, axis=(0, 1))
    attn_low = spread_rows(grad_second.astype(jnp.bfloat16))
    grad_output = jnp.einsum("sto,sti->oi", attn_low, attended, preferred_element_type=jnp.float32)
    grad_attended = jnp.einsum(
        "sto,oi->sti", attn_low, output_full, preferred_element_type=jnp.float32
    )
    grad_attended = grad_attended.astype(jnp.bfloat16).reshape(groups, local_len, heads_dev, HD)
    scores_again = (
        jnp.einsum("sqhd,skhd->shqk", query_heads, key_heads, preferred_element_type=jnp.float32)
        * scaling
    )
    probs = jnp.exp(scores_again - logsum)
    grad_probs = jnp.einsum(
        "sqhd,skhd->shqk", grad_attended, value_heads, preferred_element_type=jnp.float32
    )
    row_inner = jnp.sum(probs * grad_probs, axis=-1, keepdims=True)
    grad_scores = (probs * (grad_probs - row_inner)).astype(jnp.bfloat16)
    grad_queries = (
        jnp.einsum("shqk,skhd->sqhd", grad_scores, key_heads, preferred_element_type=jnp.float32)
        * scaling
    )
    probs_again = probs.astype(jnp.bfloat16)
    key_terms = (
        jnp.einsum("shqk,sqhd->skhd", grad_scores, query_heads, preferred_element_type=jnp.float32)
        * scaling
    )
    value_terms = jnp.einsum(
        "shqk,sqhd->skhd", probs_again, grad_attended, preferred_element_type=jnp.float32
    )
    grad_keys, grad_values = (
        lax.psum_scatter(
            key_terms.reshape(groups, seq_len, heads_dev * HD).astype(jnp.bfloat16),
            "ctx",
            scatter_dimension=1,
            tiled=True,
        ).astype(jnp.float32),
        lax.psum_scatter(
            value_terms.reshape(groups, seq_len, heads_dev * HD).astype(jnp.bfloat16),
            "ctx",
            scatter_dimension=1,
            tiled=True,
        ).astype(jnp.float32),
    )
    grad_project = jnp.stack(
        [
            grad_queries.reshape(groups, local_len, heads_dev * HD).astype(jnp.bfloat16),
            grad_keys.astype(jnp.bfloat16),
            grad_values.astype(jnp.bfloat16),
        ],
        axis=2,
    )
    grad_attend = jnp.einsum(
        "std,stcj->dcj", normed_all, grad_project, preferred_element_type=jnp.float32
    )
    grad_normed = fold_rows(
        jnp.einsum("stcj,dcj->std", grad_project, attend_full, preferred_element_type=jnp.float32)
    )
    grad_first_norm, gradient_leading_gain, grad_first_shift = first_pull(grad_normed)
    grad_joined = grad_second + grad_first_norm
    grad_merger_bias = jnp.sum(grad_joined, axis=(0, 1))
    joined_low = spread_rows(grad_joined.astype(jnp.bfloat16))
    grad_merger = jnp.einsum(
        "sto,stci->oci", joined_low, stacked, preferred_element_type=jnp.float32
    )
    grad_stacked = jnp.einsum(
        "sto,oci->stci", joined_low, merger_full, preferred_element_type=jnp.float32
    )
    expand_whole = lax.dynamic_update_slice_in_dim(
        jnp.zeros((widen_bias.shape[0],), jnp.float32), grad_expand_bias, tensor_rank * hidden, 0
    )
    weight_part = (grad_merger, grad_attend, grad_output, grad_expand, grad_shrink)
    vector_portion = (
        grad_merger_bias,
        gradient_leading_gain,
        grad_first_shift,
        grad_output_bias,
        grad_second_gain,
        grad_second_shift,
        grad_shrink_bias,
        expand_whole,
    )
    return (layer_out, grad_stacked[:, :, 0], grad_stacked[:, :, 1], weight_part, vector_portion)


def on_device(
    tokens,
    skip_tokens,
    merger_weight,
    merger_bias,
    first_gain,
    first_shift,
    attend_weight,
    output_weight,
    output_bias,
    second_gain,
    second_shift,
    expand_weight,
    widen_bias,
    shrink_weight,
    shrink_bias,
    live_slots,
    cotangent,
):
    tensor_rank = lax.axis_index("tp")
    vectors = (
        lax.all_gather(merger_bias, ("fsdp", "ctx", "tp"), axis=0, tiled=True),
        lax.all_gather(first_gain, ("fsdp", "ctx", "tp"), axis=0, tiled=True),
        lax.all_gather(first_shift, ("fsdp", "ctx", "tp"), axis=0, tiled=True),
        lax.all_gather(output_bias, ("fsdp", "ctx", "tp"), axis=0, tiled=True),
        lax.all_gather(second_gain, ("fsdp", "ctx", "tp"), axis=0, tiled=True),
        lax.all_gather(second_shift, ("fsdp", "ctx", "tp"), axis=0, tiled=True),
        lax.all_gather(shrink_bias, ("fsdp", "ctx", "tp"), axis=0, tiled=True),
        lax.all_gather(widen_bias, ("fsdp", "ctx", "tp"), axis=0, tiled=True),
    )
    batches = tokens.shape[0]
    outs_list = []
    token_list = []
    skip_list = []
    weight_totals = None
    vector_totals = None
    for batch_index in range(batches):
        current = fetch(merger_weight, attend_weight, output_weight, expand_weight, shrink_weight)
        layer_out, grad_one, gradient_remaining, weight_part, vector_portion = micro_step(
            current,
            vectors,
            tokens[batch_index],
            skip_tokens[batch_index],
            live_slots[batch_index],
            cotangent[batch_index],
            tensor_rank,
        )
        if weight_totals is None:
            weight_totals = weight_part
            vector_totals = vector_portion
        else:
            weight_totals = tuple(
                (former + latter for former, latter in zip(weight_totals, weight_part))
            )
            vector_totals = tuple(
                (former + latter for former, latter in zip(vector_totals, vector_portion))
            )
        outs_list.append(layer_out)
        token_list.append(grad_one)
        skip_list.append(gradient_remaining)
    weight_totals = reduce_weights(weight_totals)
    vector_grads = (
        lax.psum_scatter(vector_totals[0], ("fsdp", "ctx", "tp"), scatter_dimension=0, tiled=True),
        lax.psum_scatter(vector_totals[1], ("fsdp", "ctx", "tp"), scatter_dimension=0, tiled=True),
        lax.psum_scatter(vector_totals[2], ("fsdp", "ctx", "tp"), scatter_dimension=0, tiled=True),
        lax.psum_scatter(vector_totals[3], ("fsdp", "ctx", "tp"), scatter_dimension=0, tiled=True),
        lax.psum_scatter(vector_totals[4], ("fsdp", "ctx", "tp"), scatter_dimension=0, tiled=True),
        lax.psum_scatter(vector_totals[5], ("fsdp", "ctx", "tp"), scatter_dimension=0, tiled=True),
        lax.psum_scatter(vector_totals[6], ("fsdp", "ctx", "tp"), scatter_dimension=0, tiled=True),
        lax.psum_scatter(vector_totals[7], ("fsdp", "ctx", "tp"), scatter_dimension=0, tiled=True),
    )
    return (
        jnp.stack(outs_list, axis=0),
        jnp.stack(token_list, axis=0),
        jnp.stack(skip_list, axis=0),
        weight_totals[0],
        vector_grads[0],
        vector_grads[1],
        vector_grads[2],
        weight_totals[1],
        weight_totals[2],
        vector_grads[3],
        vector_grads[4],
        vector_grads[5],
        weight_totals[3],
        vector_grads[7],
        weight_totals[4],
        vector_grads[6],
    )


def solution(mesh):
    placed = (
        P(None, "fsdp", "ctx", "tp"),
        P(None, "fsdp", "ctx", "tp"),
        P(("fsdp", "ctx"), None, "tp"),
        P(("fsdp", "ctx", "tp")),
        P(("fsdp", "ctx", "tp")),
        P(("fsdp", "ctx", "tp")),
        P(("fsdp", "ctx"), None, "tp"),
        P(("fsdp", "ctx"), "tp"),
        P(("fsdp", "ctx", "tp")),
        P(("fsdp", "ctx", "tp")),
        P(("fsdp", "ctx", "tp")),
        P(("fsdp", "ctx"), "tp"),
        P(("fsdp", "ctx", "tp")),
        P(("fsdp", "ctx"), "tp"),
        P(("fsdp", "ctx", "tp")),
        P(None, "fsdp"),
        P(None, "fsdp", ("ctx", "tp"), None),
    )
    return jax.shard_map(
        on_device,
        mesh=mesh,
        in_specs=placed,
        out_specs=(
            P(None, "fsdp", ("ctx", "tp"), None),
            P(None, "fsdp", "ctx", "tp"),
            P(None, "fsdp", "ctx", "tp"),
            P(("fsdp", "ctx"), None, "tp"),
            P(("fsdp", "ctx", "tp")),
            P(("fsdp", "ctx", "tp")),
            P(("fsdp", "ctx", "tp")),
            P(("fsdp", "ctx"), None, "tp"),
            P(("fsdp", "ctx"), "tp"),
            P(("fsdp", "ctx", "tp")),
            P(("fsdp", "ctx", "tp")),
            P(("fsdp", "ctx", "tp")),
            P(("fsdp", "ctx"), "tp"),
            P(("fsdp", "ctx", "tp")),
            P(("fsdp", "ctx"), "tp"),
            P(("fsdp", "ctx", "tp")),
        ),
        check_vma=False,
    )
```

profile of v0, /device:TPU:0, one launch (start us, length us, event | category | flops | bytes accessed | tf_op | source)
XLA Modules:
  0.0 2147.7 jit_solution(7706245499468301437)
XLA Ops:
  10.6 43.0 %all-gather.42.cloned.1.call-done = bf16[1024,2,256]{2,0,1:T(8,128)(2,1)} async-done(((bf16[128,2,256]{2,0,1:T(8,128)(2,1)}), bf16[1024,2,256]{2,0,1:T(8,128)(2,1)}) %all-gather.42.cloned.1.call-update) | async-done | bytes 1048592 | tf_op jit(solution)/shard_map/all_gather | solution.py:22
  66.0 38.9 %all-reduce.16 = (f32[1024]{0:T(1024)S(1)}, f32[1024]{0:T(1024)S(1)}, f32[1024]{0:T(1024)S(1)}, f32[1024]{0:T(1024)S(1)}, f32[1024]{0:T(1024)S(1)}, /*index=5*/f32[1024]{0:T(1024)S(1)}) all-reduce(f32[1024]{0:T(1024)S(1)} %dynamic-update-slice.3, ...), channel_id=1, replica_groups=mesh['fsdp'=2,'ctx'=4,'tp'=4] {'fsdp','ctx','tp'}, use_global_device_ids=true, to_apply=%add | all-reduce | flops 6144 | bytes 49152
  122.3 33.8 %reduce-scatter.46.cloned.1.call-done = f32[2,64,1024]{2,1,0:T(8,128)} async-done(((f32[2,256,1024]{2,1,0:T(8,128)}), f32[2,64,1024]{2,1,0:T(8,128)}) %reduce-scatter.46.cloned.1.call-update) | async-done | bytes 524304 | tf_op jit(solution)/shard_map/reduce_scatter | solution.py:35
  156.1 34.0 %reduce-scatter.52.cloned.1.call-done = f32[2,64,1024]{2,1,0:T(8,128)} async-done(((f32[2,256,1024]{2,1,0:T(8,128)}), f32[2,64,1024]{2,1,0:T(8,128)}) %reduce-scatter.52.cloned.1.call-update) | async-done | bytes 524304 | tf_op jit(solution)/shard_map/reduce_scatter | solution.py:35
  196.6 41.2 %all-gather.46.cloned.1.call-done = bf16[1024,3,256]{0,2,1:T(8,128)(2,1)} async-done(((bf16[128,3,256]{0,2,1:T(8,128)(2,1)}), bf16[1024,3,256]{0,2,1:T(8,128)(2,1)}) %all-gather.46.cloned.1.call-update) | async-done | bytes 1572880 | tf_op jit(solution)/shard_map/all_gather | solution.py:23
  315.2 34.9 %all_gather.146 = bf16[1024,256]{1,0:T(8,128)(2,1)S(1)} all-gather(bf16[128,256]{1,0:T(8,128)(2,1)S(1)} %copy-done.113), channel_id=1, replica_groups=mesh['fsdp'=2,'ctx'=4,'tp'=4] {'fsdp','ctx'}, dimensions={0}, use_global_device_ids=true | all-gather | bytes 589824 | tf_op jit(solution)/shard_map/all_gather | solution.py:24
  356.6 24.6 %all-gather.94.cloned.1.call-done = bf16[2,1024,1,256]{1,3,2,0:T(8,128)(2,1)} async-done(((bf16[2,256,1,256]{1,3,2,0:T(8,128)(2,1)}), bf16[2,1024,1,256]{1,3,2,0:T(8,128)(2,1)}) %all-gather.94.cloned.1.call-update) | async-done | bytes 1048592 | tf_op jit(solution)/shard_map/all_gather | solution.py:79
  571.4 24.9 %reduce-scatter.42.cloned.1.call-done = f32[2,64,1024]{2,1,0:T(8,128)} async-done(((f32[2,256,1024]{2,1,0:T(8,128)}), f32[2,64,1024]{2,1,0:T(8,128)}) %reduce-scatter.42.cloned.1.call-update) | async-done | bytes 524304 | tf_op jit(solution)/shard_map/reduce_scatter | solution.py:35
  596.2 34.6 %reduce-scatter.48.cloned.1.call-done = f32[2,64,1024]{2,1,0:T(8,128)} async-done(((f32[2,256,1024]{2,1,0:T(8,128)}), f32[2,64,1024]{2,1,0:T(8,128)}) %reduce-scatter.48.cloned.1.call-update) | async-done | bytes 524304 | tf_op jit(solution)/shard_map/reduce_scatter | solution.py:35
  630.8 34.0 %reduce-scatter.54.cloned.1.call-done = f32[2,64,1024]{2,1,0:T(8,128)} async-done(((f32[2,256,1024]{2,1,0:T(8,128)}), f32[2,64,1024]{2,1,0:T(8,128)}) %reduce-scatter.54.cloned.1.call-update) | async-done | bytes 524304 | tf_op jit(solution)/shard_map/reduce_scatter | solution.py:35
  664.8 34.2 %reduce-scatter.36.cloned.1.call-done = f32[2,64,1024]{2,1,0:T(8,128)} async-done(((f32[2,256,1024]{2,1,0:T(8,128)}), f32[2,64,1024]{2,1,0:T(8,128)}) %reduce-scatter.36.cloned.1.call-update) | async-done | bytes 524304 | tf_op jit(solution)/shard_map/reduce_scatter | solution.py:35
  711.8 41.1 %all-gather.8 = f32[32,1,128]{2,1,0:T(1,128)S(1)} all-gather(f32[1,1,128]{2,1,0:T(1,128)S(1)} %bitcast.612), channel_id=1, replica_groups=mesh['fsdp'=2,'ctx'=4,'tp'=4] {'fsdp','ctx','tp'}, dimensions={0}, use_global_device_ids=true | all-gather | bytes 16896 | tf_op jit(solution)/shard_map/all_gather | solution.py:254
  855.1 38.8 %all-gather.52.cloned.1.call-done = bf16[1024,1024]{1,0:T(8,128)(2,1)} async-done(((bf16[128,1024]{1,0:T(8,128)(2,1)}), bf16[1024,1024]{1,0:T(8,128)(2,1)}) %all-gather.52.cloned.1.call-update) | async-done | bytes 2097168 | tf_op jit(solution)/shard_map/all_gather | solution.py:26
  956.7 24.9 %reduce-scatter.82.cloned.1.call-done = f32[2,64,1024]{2,1,0:T(8,128)} async-done(((f32[2,256,1024]{2,1,0:T(8,128)}), f32[2,64,1024]{2,1,0:T(8,128)}) %reduce-scatter.82.cloned.1.call-update) | async-done | bytes 524304 | tf_op jit(solution)/shard_map/reduce_scatter | solution.py:35
  983.5 32.9 %reduce-scatter.74.cloned.1.call-done = f32[2,64,1024]{2,1,0:T(8,128)} async-done(((f32[2,256,1024]{2,1,0:T(8,128)}), f32[2,64,1024]{2,1,0:T(8,128)}) %reduce-scatter.74.cloned.1.call-update) | async-done | bytes 524304 | tf_op jit(solution)/shard_map/reduce_scatter | solution.py:35
  1016.4 34.0 %reduce-scatter.66.cloned.1.call-done = f32[2,64,1024]{2,1,0:T(8,128)} async-done(((f32[2,256,1024]{2,1,0:T(8,128)}), f32[2,64,1024]{2,1,0:T(8,128)}) %reduce-scatter.66.cloned.1.call-update) | async-done | bytes 524304 | tf_op jit(solution)/shard_map/reduce_scatter | solution.py:35
  1050.3 34.0 %reduce-scatter.58.cloned.1.call-done = f32[2,64,1024]{2,1,0:T(8,128)} async-done(((f32[2,256,1024]{2,1,0:T(8,128)}), f32[2,64,1024]{2,1,0:T(8,128)}) %reduce-scatter.58.cloned.1.call-update) | async-done | bytes 524304 | tf_op jit(solution)/shard_map/reduce_scatter | solution.py:35
  1196.5 24.9 %reduce-scatter.84.cloned.1.call-done = bf16[2,256,256]{2,1,0:T(8,128)(2,1)} async-done(((bf16[2,1024,256]{2,1,0:T(8,128)(2,1)}), bf16[2,256,256]{2,1,0:T(8,128)(2,1)}) %reduce-scatter.84.cloned.1.call-update) | async-done | bytes 262160 | tf_op jit(solution)/shard_map/reduce_scatter | solution.py:172
  1249.3 28.2 %reduce-scatter.68.cloned.1.call-done = bf16[2,256,256]{2,1,0:T(8,128)(2,1)} async-done(((bf16[2,1024,256]{2,1,0:T(8,128)(2,1)}), bf16[2,256,256]{2,1,0:T(8,128)(2,1)}) %reduce-scatter.68.cloned.1.call-update) | async-done | bytes 262160 | tf_op jit(solution)/shard_map/reduce_scatter | solution.py:172
  1305.5 28.0 %reduce-scatter.60.cloned.1.call-done = bf16[2,256,256]{2,1,0:T(8,128)(2,1)} async-done(((bf16[2,1024,256]{2,1,0:T(8,128)(2,1)}), bf16[2,256,256]{2,1,0:T(8,128)(2,1)}) %reduce-scatter.60.cloned.1.call-update) | async-done | bytes 262160 | tf_op jit(solution)/shard_map/reduce_scatter | solution.py:172
  1361.5 28.1 %reduce-scatter.76.cloned.1.call-done = bf16[2,256,256]{2,1,0:T(8,128)(2,1)} async-done(((bf16[2,1024,256]{2,1,0:T(8,128)(2,1)}), bf16[2,256,256]{2,1,0:T(8,128)(2,1)}) %reduce-scatter.76.cloned.1.call-update) | async-done | bytes 262160 | tf_op jit(solution)/shard_map/reduce_scatter | solution.py:172
  1393.7 28.9 %reduce-scatter.88.cloned.1.call-done = f32[2,64,1024]{2,1,0:T(8,128)} async-done(((f32[2,256,1024]{2,1,0:T(8,128)}), f32[2,64,1024]{2,1,0:T(8,128)}) %reduce-scatter.88.cloned.1.call-update) | async-done | bytes 524304 | tf_op jit(solution)/shard_map/reduce_scatter | solution.py:35
  1422.7 34.7 %reduce-scatter.72.cloned.1.call-done = f32[2,64,1024]{2,1,0:T(8,128)} async-done(((f32[2,256,1024]{2,1,0:T(8,128)}), f32[2,64,1024]{2,1,0:T(8,128)}) %reduce-scatter.72.cloned.1.call-update) | async-done | bytes 524304 | tf_op jit(solution)/shard_map/reduce_scatter | solution.py:35
  1457.4 33.8 %reduce-scatter.64.cloned.1.call-done = f32[2,64,1024]{2,1,0:T(8,128)} async-done(((f32[2,256,1024]{2,1,0:T(8,128)}), f32[2,64,1024]{2,1,0:T(8,128)}) %reduce-scatter.64.cloned.1.call-update) | async-done | bytes 524304 | tf_op jit(solution)/shard_map/reduce_scatter | solution.py:35
  1491.2 34.2 %reduce-scatter.80.cloned.1.call-done = f32[2,64,1024]{2,1,0:T(8,128)} async-done(((f32[2,256,1024]{2,1,0:T(8,128)}), f32[2,64,1024]{2,1,0:T(8,128)}) %reduce-scatter.80.cloned.1.call-update) | async-done | bytes 524304 | tf_op jit(solution)/shard_map/reduce_scatter | solution.py:35
  1645.5 40.4 %all-reduce.15 = (f32[1024]{0:T(1024)S(1)}, f32[1024]{0:T(1024)S(1)}, f32[1024]{0:T(1024)S(1)}, f32[1024]{0:T(1024)S(1)}, f32[1024]{0:T(1024)S(1)}, /*index=5*/f...) all-reduce(f32[1024]{0:T(1024)S(1)} %dynamic-update-slice.9, ...), channel_id=1, replica_groups=mesh['fsdp'=2,'ctx'=4,'tp'=4] {'fsdp','ctx','tp'}, use_global_device_ids=true, to_apply=%add.6 | all-reduce | flops 12288 | bytes 98304
  1706.5 34.2 %reduce-scatter.56.cloned.1.call-done = f32[2,64,1024]{2,1,0:T(8,128)} async-done(((f32[2,256,1024]{2,1,0:T(8,128)}), f32[2,64,1024]{2,1,0:T(8,128)}) %reduce-scatter.56.cloned.1.call-update) | async-done | bytes 524304 | tf_op jit(solution)/shard_map/reduce_scatter | solution.py:35
  1752.1 59.7 %reduce-scatter.90.cloned.1.call-done = f32[128,2,256]{2,0,1:T(8,128)} async-done(((f32[1024,2,256]{2,0,1:T(8,128)}), f32[128,2,256]{2,0,1:T(8,128)}) %reduce-scatter.90.cloned.1.call-update) | async-done | bytes 262160 | tf_op jit(solution)/shard_map/reduce_scatter | solution.py:40
  1813.7 64.7 %reduce-scatter.94.cloned.1.call-done = f32[128,256]{1,0:T(8,128)} async-done(((f32[1024,256]{1,0:T(8,128)}), f32[128,256]{1,0:T(8,128)}) %reduce-scatter.94.cloned.1.call-update) | async-done | bytes 131088 | tf_op jit(solution)/shard_map/reduce_scatter | solution.py:42
  1878.3 91.6 %reduce-scatter.96.cloned.1.call-done = f32[128,1024]{1,0:T(8,128)} async-done(((f32[1024,1024]{1,0:T(8,128)}), f32[128,1024]{1,0:T(8,128)}) %reduce-scatter.96.cloned.1.call-update) | async-done | bytes 524304 | tf_op jit(solution)/shard_map/reduce_scatter | solution.py:43
  1969.9 91.7 %reduce-scatter.98.cloned.1.call-done = f32[128,1024]{1,0:T(8,128)} async-done(((f32[1024,1024]{1,0:T(8,128)}), f32[128,1024]{1,0:T(8,128)}) %reduce-scatter.98.cloned.1.call-update) | async-done | bytes 524304 | tf_op jit(solution)/shard_map/reduce_scatter | solution.py:44
  2061.6 79.3 %reduce-scatter.92.cloned.1.call-done = f32[128,3,256]{2,0,1:T(8,128)} async-done(((f32[1024,3,256]{2,0,1:T(8,128)}), f32[128,3,256]{2,0,1:T(8,128)}) %reduce-scatter.92.cloned.1.call-update) | async-done | bytes 393232 | tf_op jit(solution)/shard_map/reduce_scatter | solution.py:41
  (769 shorter events, 844.1 us)
Async XLA Ops:
  63.6 174.2 %all-gather.46.cloned.1.call-start = ((), (), s32[]{:S(2)}) async-start(), calls=%async_computation.36 | async-start | bytes 1769472 | tf_op jit(solution)/shard_map/all_gather | solution.py:23
  64.5 190.4 %all-gather.54.cloned.1.call-start = ((), (), s32[]{:S(2)}) async-start(), calls=%async_computation.43 | async-start | bytes 1310720 | tf_op jit(solution)/shard_map/all_gather | solution.py:31
  277.4 165.0 %all-gather.98.cloned.1.call-start = ((), (), s32[]{:S(2)}) async-start(), calls=%async_computation.94 | async-start | bytes 1310720 | tf_op jit(solution)/shard_map/all_gather | solution.py:79
  278.0 194.9 %all-gather.104.cloned.1.call-start = ((), (), s32[]{:S(2)}) async-start(), calls=%async_computation.97 | async-start | bytes 1310720 | tf_op jit(solution)/shard_map/all_gather | solution.py:78
  296.4 206.6 %all-gather.102.cloned.1.call-start = ((), (), s32[]{:S(2)}) async-start(), calls=%async_computation.96 | async-start | bytes 1310720 | tf_op jit(solution)/shard_map/all_gather | solution.py:79
  296.9 236.5 %all-gather.92.cloned.1.call-start = ((), (), s32[]{:S(2)}) async-start(), calls=%async_computation.91 | async-start | bytes 1310720 | tf_op jit(solution)/shard_map/all_gather | solution.py:78
  315.1 248.3 %all-gather.90.cloned.1.call-start = ((), (), s32[]{:S(2)}) async-start(), calls=%async_computation.90 | async-start | bytes 1310720 | tf_op jit(solution)/shard_map/all_gather | solution.py:79
  350.1 246.2 %reduce-scatter.42.cloned.1.call-start = ((), (), s32[]{:S(2)}) async-start(), calls=%async_computation.44 | async-start | bytes 2621440 | tf_op jit(solution)/shard_map/reduce_scatter | solution.py:35
  388.4 242.4 %reduce-scatter.48.cloned.1.call-start = ((), (), s32[]{:S(2)}) async-start(), calls=%async_computation.49 | async-start | bytes 2621440 | tf_op jit(solution)/shard_map/reduce_scatter | solution.py:35
  449.6 215.2 %reduce-scatter.54.cloned.1.call-start = ((), (), s32[]{:S(2)}) async-start(), calls=%async_computation.54 | async-start | bytes 2621440 | tf_op jit(solution)/shard_map/reduce_scatter | solution.py:35
  510.1 188.9 %reduce-scatter.36.cloned.1.call-start = ((), (), s32[]{:S(2)}) async-start(), calls=%async_computation.37 | async-start | bytes 2621440 | tf_op jit(solution)/shard_map/reduce_scatter | solution.py:35
  570.6 182.3 %all-gather.50.cloned.1.call-start = ((), (), s32[]{:S(2)}) async-start(), calls=%async_computation.39 | async-start | bytes 2359296 | tf_op jit(solution)/shard_map/all_gather | solution.py:25
  571.3 196.4 %all-gather.60.cloned.1.call-start = ((), (), s32[]{:S(2)}) async-start(), calls=%async_computation.50 | async-start | bytes 1310720 | tf_op jit(solution)/shard_map/all_gather | solution.py:31
  709.0 184.9 %all-gather.52.cloned.1.call-start = ((), (), s32[]{:S(2)}) async-start(), calls=%async_computation.40 | async-start | bytes 2359296 | tf_op jit(solution)/shard_map/all_gather | solution.py:26
  709.7 200.8 %all-gather.78.cloned.1.call-start = ((), (), s32[]{:S(2)}) async-start(), calls=%async_computation.71 | async-start | bytes 1310720 | tf_op jit(solution)/shard_map/all_gather | solution.py:31
  710.3 218.6 %all-gather.72.cloned.1.call-start = ((), (), s32[]{:S(2)}) async-start(), calls=%async_computation.64 | async-start | bytes 1310720 | tf_op jit(solution)/shard_map/all_gather | solution.py:31
  711.0 236.2 %all-gather.66.cloned.1.call-start = ((), (), s32[]{:S(2)}) async-start(), calls=%async_computation.57 | async-start | bytes 1310720 | tf_op jit(solution)/shard_map/all_gather | solution.py:31
  711.8 269.8 %reduce-scatter.82.cloned.1.call-start = ((), (), s32[]{:S(2)}) async-start(), calls=%async_computation.79 | async-start | bytes 2621440 | tf_op jit(solution)/shard_map/reduce_scatter | solution.py:35
  1158.4 175.1 %reduce-scatter.60.cloned.1.call-start = ((), (), s32[]{:S(2)}) async-start(), calls=%async_computation.60 | async-start | bytes 1310720 | tf_op jit(solution)/shard_map/reduce_scatter | solution.py:172
  1171.3 190.2 %reduce-scatter.78.cloned.1.call-start = ((), (), s32[]{:S(2)}) async-start(), calls=%async_computation.75 | async-start | bytes 1310720 | tf_op jit(solution)/shard_map/reduce_scatter | solution.py:178
  1179.7 209.9 %reduce-scatter.76.cloned.1.call-start = ((), (), s32[]{:S(2)}) async-start(), calls=%async_computation.74 | async-start | bytes 1310720 | tf_op jit(solution)/shard_map/reduce_scatter | solution.py:172
  1192.6 230.0 %reduce-scatter.88.cloned.1.call-start = ((), (), s32[]{:S(2)}) async-start(), calls=%async_computation.83 | async-start | bytes 2621440 | tf_op jit(solution)/shard_map/reduce_scatter | solution.py:35
  1225.2 232.2 %reduce-scatter.72.cloned.1.call-start = ((), (), s32[]{:S(2)}) async-start(), calls=%async_computation.69 | async-start | bytes 2621440 | tf_op jit(solution)/shard_map/reduce_scatter | solution.py:35
  1281.4 209.8 %reduce-scatter.64.cloned.1.call-start = ((), (), s32[]{:S(2)}) async-start(), calls=%async_computation.62 | async-start | bytes 2621440 | tf_op jit(solution)/shard_map/reduce_scatter | solution.py:35
  1337.5 187.9 %reduce-scatter.80.cloned.1.call-start = ((), (), s32[]{:S(2)}) async-start(), calls=%async_computation.76 | async-start | bytes 2621440 | tf_op jit(solution)/shard_map/reduce_scatter | solution.py:35
  1544.3 162.2 %reduce-scatter.50.cloned.1.call-start = ((), (), s32[]{:S(2)}) async-start(), calls=%async_computation.51 | async-start | bytes 2621440 | tf_op jit(solution)/shard_map/reduce_scatter | solution.py:35
  1548.1 192.5 %reduce-scatter.56.cloned.1.call-start = ((), (), s32[]{:S(2)}) async-start(), calls=%async_computation.56 | async-start | bytes 2621440 | tf_op jit(solution)/shard_map/reduce_scatter | solution.py:35
  1552.0 259.8 %reduce-scatter.90.cloned.1.call-start = ((), (), s32[]{:S(2)}) async-start(), calls=%async_computation.85 | async-start | bytes 2359296 | tf_op jit(solution)/shard_map/reduce_scatter | solution.py:40
  1608.8 269.6 %reduce-scatter.94.cloned.1.call-start = ((), (), s32[]{:S(2)}) async-start(), calls=%async_computation.87 | async-start | bytes 1179648 | tf_op jit(solution)/shard_map/reduce_scatter | solution.py:42
  1615.1 354.7 %reduce-scatter.96.cloned.1.call-start = ((), (), s32[]{:S(2)}) async-start(), calls=%async_computation.88 | async-start | bytes 4718592 | tf_op jit(solution)/shard_map/reduce_scatter | solution.py:43
  1624.7 436.9 %reduce-scatter.98.cloned.1.call-start = ((), (), s32[]{:S(2)}) async-start(), calls=%async_computation.89 | async-start | bytes 4718592 | tf_op jit(solution)/shard_map/reduce_scatter | solution.py:44
  1635.1 505.9 %reduce-scatter.92.cloned.1.call-start = ((), (), s32[]{:S(2)}) async-start(), calls=%async_computation.86 | async-start | bytes 3538944 | tf_op jit(solution)/shard_map/reduce_scatter | solution.py:41
  (226 other events, 11546.0 us)
Sparse Core Ops, SparseCore 0:
  10.7 42.8 all-gather.41
  57.1 30.3 reduce-scatter.33
  90.8 31.4 reduce-scatter.39
  124.7 31.3 reduce-scatter.45
  158.6 31.4 reduce-scatter.51
  192.5 45.3 all-gather.45
  313.6 37.0 all-gather.95
  352.7 28.5 all-gather.93
  504.9 28.4 all-gather.91
  566.5 29.7 reduce-scatter.41
  599.3 31.4 reduce-scatter.47
  633.4 31.3 reduce-scatter.53
  667.5 31.4 reduce-scatter.35
  701.1 49.2 all-gather.49
  844.6 49.2 all-gather.51
  950.2 31.4 reduce-scatter.81
  984.9 31.4 reduce-scatter.73
  1018.9 31.4 reduce-scatter.65
  1052.9 31.4 reduce-scatter.57
  1392.6 30.0 reduce-scatter.87
  1425.9 31.4 reduce-scatter.71
  1459.8 31.4 reduce-scatter.63
  1493.9 31.4 reduce-scatter.79
  1606.5 31.4 reduce-scatter.37
  1641.1 31.5 reduce-scatter.43
  1675.1 31.3 reduce-scatter.49
  1709.2 31.4 reduce-scatter.55
  1744.2 67.5 reduce-scatter.89
  1815.8 62.4 reduce-scatter.93
  1882.8 87.0 reduce-scatter.95
  1973.9 87.6 reduce-scatter.97
  2066.2 74.6 reduce-scatter.91
  (33 shorter events, 677.9 us)
where the time goes:
time: 2160 us; the launch traced here: 2150 us
  waiting for transfers between devices  1570 us (73%)
  matrix products  256 us (12%)
  blocking collectives  155 us (7%)
  other arithmetic  86.4 us (4%)
  local copies, waits for them, and re-layouts  58.5 us (3%)
    reduce_scatter x20, waiting for transfers between devices, fold_rows(): return lax.psum_scatter(block, 'tp', scatter_dimension=1, tiled=True)  519 us
    all_gather x20, waiting for transfers between devices, spread_rows(): return lax.all_gather(block, 'tp', axis=1, tiled=True)  196 us
    reduce_scatter x4, waiting for transfers between devices, micro_step(): lax.psum_scatter(key_terms.reshape(groups, seq_len, heads_dev * HD).astyp...  109 us
    all_gather x4, waiting for transfers between devices, micro_step(): lax.all_gather(project[:, :, 2], 'ctx', axis=1, tiled=True)  97.3 us
    reduce_scatter x1, waiting for transfers between devices, reduce_weights(): lax.psum_scatter(parts[4], ('fsdp', 'ctx'), scatter_dimension=0, tiled=True)  91.7 us
    reduce_scatter x1, waiting for transfers between devices, reduce_weights(): lax.psum_scatter(parts[3], ('fsdp', 'ctx'), scatter_dimension=0, tiled=True)  91.6 us
    reduce_scatter x1, waiting for transfers between devices, reduce_weights(): lax.psum_scatter(parts[1], ('fsdp', 'ctx'), scatter_dimension=0, tiled=True)  79.3 us
    unnamed x2, blocking collectives  79.3 us
  transfers between devices with their start and end apart: 65, of which 55 were waited for; matrix products, arithmetic and copies ran while one was open for 16% of the time, Pallas kernels for 0%

commit v1 on v0

--- a/solution.py
+++ b/solution.py
@@ -5,6 +5,18 @@
 
 HD = 64
 EPSILON = 1e-05
+
+
+def gather_by_bits(shard, axis, dim):
+    ways, here = (lax.axis_size(axis), lax.axis_index(axis))
+    grown, reach = (shard, 1)
+    while reach < ways:
+        theirs = lax.ppermute(grown, axis, [(d, d ^ reach) for d in range(ways)])
+        mine_first = jnp.concatenate([grown, theirs], axis=dim)
+        theirs_first = jnp.concatenate([theirs, grown], axis=dim)
+        grown = jnp.where(here & reach == 0, mine_first, theirs_first)
+        reach = 2 * reach
+    return grown
 
 
 def layer_norm(matrix, scales, shifts):
@@ -75,7 +87,7 @@
         "std,dcj->stcj", normed_all, attend_full, preferred_element_type=jnp.float32
     ).astype(jnp.bfloat16)
     key_rows, value_rows = (
-        lax.all_gather(project[:, :, 1], "ctx", axis=1, tiled=True),
+        gather_by_bits(project[:, :, 1], "ctx", 1),
         lax.all_gather(project[:, :, 2], "ctx", axis=1, tiled=True),
     )
     seq_len = key_rows.shape[1]

time: 2160 us -> 2080 us (0.963)
  waiting for transfers between devices: 1570 us -> 1480 us
    ppermute x0 -> x8, waiting for transfers between devices: none -> 153 us  [gather_by_bits(): theirs = lax.ppermute(grown, axis, [(d, d ^ reach) for d in range(ways)])]
    all_gather x4, waiting for transfers between devices: 97.3 us -> 0.01 us  [micro_step(): lax.all_gather(project[:, :, 2], 'ctx', axis=1, tiled=True)]
    all_gather x4 -> x0, waiting for transfers between devices: 70.1 us -> none  [micro_step(): lax.all_gather(project[:, :, 1], 'ctx', axis=1, tiled=True)]
    reduce_scatter x20, waiting for transfers between devices: 519 us -> 459 us  [fold_rows(): return lax.psum_scatter(block, 'tp', scatter_dimension=1, tiled=True)]
  transfers between devices with their start and end apart: 65 -> 69, of which waited for: 55 -> 51; matrix products, arithmetic and copies ran while one was open for 16% -> 17% of each run, Pallas kernels for 0% -> 0%
where the time goes in v1:
time: 2080 us; the launch traced here: 2070 us
  waiting for transfers between devices  1480 us (71%)
  matrix products  252 us (12%)
  blocking collectives  158 us (8%)
  other arithmetic  90.2 us (4%)
  local copies, waits for them, and re-layouts  58.3 us (3%)
    reduce_scatter x20, waiting for transfers between devices, fold_rows(): return lax.psum_scatter(block, 'tp', scatter_dimension=1, tiled=True)  459 us
    all_gather x20, waiting for transfers between devices, spread_rows(): return lax.all_gather(block, 'tp', axis=1, tiled=True)  183 us
    ppermute x8, waiting for transfers between devices, gather_by_bits(): theirs = lax.ppermute(grown, axis, [(d, d ^ reach) for d in range(ways)])  153 us
    reduce_scatter x4, waiting for transfers between devices, micro_step(): lax.psum_scatter(key_terms.reshape(groups, seq_len, heads_dev * HD).astyp...  109 us
    reduce_scatter x1, waiting for transfers between devices, reduce_weights(): lax.psum_scatter(parts[4], ('fsdp', 'ctx'), scatter_dimension=0, tiled=True)  91.9 us
    reduce_scatter x1, waiting for transfers between devices, reduce_weights(): lax.psum_scatter(parts[3], ('fsdp', 'ctx'), scatter_dimension=0, tiled=True)  91.4 us
    reduce_scatter x1, waiting for transfers between devices, reduce_weights(): lax.psum_scatter(parts[1], ('fsdp', 'ctx'), scatter_dimension=0, tiled=True)  79.4 us
    unnamed x2, blocking collectives  79.2 us
  transfers between devices with their start and end apart: 69, of which 51 were waited for; matrix products, arithmetic and copies ran while one was open for 17% of the time, Pallas kernels for 0%

profile of v1, /device:TPU:0, one launch (start us, length us, event | category | flops | bytes accessed | tf_op | source)
XLA Modules:
  0.0 2067.9 jit_solution(2710852898366245291)
XLA Ops:
  10.6 43.0 %all-gather.34.cloned.1.call-done = bf16[1024,2,256]{2,0,1:T(8,128)(2,1)} async-done(((bf16[128,2,256]{2,0,1:T(8,128)(2,1)}), bf16[1024,2,256]{2,0,1:T(8,128)(2,1)}) %all-gather.34.cloned.1.call-update) | async-done | bytes 1048592 | tf_op jit(solution)/shard_map/all_gather | solution.py:34
  65.9 38.9 %all-reduce.16 = (f32[1024]{0:T(1024)S(1)}, f32[1024]{0:T(1024)S(1)}, f32[1024]{0:T(1024)S(1)}, f32[1024]{0:T(1024)S(1)}, f32[1024]{0:T(1024)S(1)}, /*index=5*/f32[1024]{0:T(1024)S(1)}) all-reduce(f32[1024]{0:T(1024)S(1)} %dynamic-update-slice.3, ...), channel_id=1, replica_groups=mesh['fsdp'=2,'ctx'=4,'tp'=4] {'fsdp','ctx','tp'}, use_global_device_ids=true, to_apply=%add | all-reduce | flops 6144 | bytes 49152
  122.3 33.8 %reduce-scatter.46.cloned.1.call-done = f32[2,64,1024]{2,1,0:T(8,128)} async-done(((f32[2,256,1024]{2,1,0:T(8,128)}), f32[2,64,1024]{2,1,0:T(8,128)}) %reduce-scatter.46.cloned.1.call-update) | async-done | bytes 524304 | tf_op jit(solution)/shard_map/reduce_scatter | solution.py:47
  156.1 34.0 %reduce-scatter.52.cloned.1.call-done = f32[2,64,1024]{2,1,0:T(8,128)} async-done(((f32[2,256,1024]{2,1,0:T(8,128)}), f32[2,64,1024]{2,1,0:T(8,128)}) %reduce-scatter.52.cloned.1.call-update) | async-done | bytes 524304 | tf_op jit(solution)/shard_map/reduce_scatter | solution.py:47
  196.7 41.3 %all-gather.38.cloned.1.call-done = bf16[1024,3,256]{0,2,1:T(8,128)(2,1)} async-done(((bf16[128,3,256]{0,2,1:T(8,128)(2,1)}), bf16[1024,3,256]{0,2,1:T(8,128)(2,1)}) %all-gather.38.cloned.1.call-update) | async-done | bytes 1572880 | tf_op jit(solution)/shard_map/all_gather | solution.py:35
  298.0 37.6 %all_gather.133 = bf16[1024,256]{1,0:T(8,128)(2,1)S(1)} all-gather(bf16[128,256]{1,0:T(8,128)(2,1)S(1)} %copy-done.126), channel_id=1, replica_groups=mesh['fsdp'=2,'ctx'=4,'tp'=4] {'fsdp','ctx'}, dimensions={0}, use_global_device_ids=true | all-gather | bytes 589824 | tf_op jit(solution)/shard_map/all_gather | solution.py:36
  341.6 24.8 %collective-permute-done.3 = bf16[2,512,256]{1,2,0:T(8,128)(2,1)} collective-permute-done((bf16[2,512,256]{1,2,0:T(8,128)(2,1)}, bf16[2,512,256]{1,2,0:T(8,128)(2,1)}, u32[]{:S(2)}, u32[]{:S(2)}) %collective-permute-start.3) | collective-permute-done | bytes 524320 | tf_op jit(solution)/shard_map/ppermute | solution.py:14
  396.1 40.1 %collective-permute-done.5 = bf16[2,512,256]{1,2,0:T(8,128)(2,1)S(1)} collective-permute-done((bf16[2,512,256]{1,2,0:T(8,128)(2,1)S(1)}, bf16[2,512,256]{1,2,0:T(8,128)(2,1)S(1)}, u32[]{:S(2)}, u32[]{:S(2)}) %collective-permute-start.5) | collective-permute-done | bytes 524320 | tf_op jit(solution)/shard_map/ppermute | solution.py:14
  466.8 26.3 %collective-permute-done.7 = bf16[2,512,256]{1,2,0:T(8,128)(2,1)S(1)} collective-permute-done((bf16[2,512,256]{1,2,0:T(8,128)(2,1)S(1)}, bf16[2,512,256]{1,2,0:T(8,128)(2,1)S(1)}, u32[]{:S(2)}, u32[]{:S(2)}) %collective-permute-start.7) | collective-permute-done | bytes 524320 | tf_op jit(solution)/shard_map/ppermute | solution.py:14
  513.6 24.9 %collective-permute-done.1 = bf16[2,512,256]{1,2,0:T(8,128)(2,1)S(1)} collective-permute-done((bf16[2,512,256]{1,2,0:T(8,128)(2,1)S(1)}, bf16[2,512,256]{1,2,0:T(8,128)(2,1)S(1)}, u32[]{:S(2)}, u32[]{:S(2)}) %collective-permute-start.1) | collective-permute-done | bytes 524320 | tf_op jit(solution)/shard_map/ppermute | solution.py:14
  551.3 33.1 %reduce-scatter.54.cloned.1.call-done = f32[2,64,1024]{2,1,0:T(8,128)} async-done(((f32[2,256,1024]{2,1,0:T(8,128)}), f32[2,64,1024]{2,1,0:T(8,128)}) %reduce-scatter.54.cloned.1.call-update) | async-done | bytes 524304 | tf_op jit(solution)/shard_map/reduce_scatter | solution.py:47
  584.4 34.0 %reduce-scatter.36.cloned.1.call-done = f32[2,64,1024]{2,1,0:T(8,128)} async-done(((f32[2,256,1024]{2,1,0:T(8,128)}), f32[2,64,1024]{2,1,0:T(8,128)}) %reduce-scatter.36.cloned.1.call-update) | async-done | bytes 524304 | tf_op jit(solution)/shard_map/reduce_scatter | solution.py:47
  631.4 41.2 %all-gather.4 = f32[32,1,128]{2,1,0:T(1,128)S(1)} all-gather(f32[1,1,128]{2,1,0:T(1,128)S(1)} %bitcast.622), channel_id=1, replica_groups=mesh['fsdp'=2,'ctx'=4,'tp'=4] {'fsdp','ctx','tp'}, dimensions={0}, use_global_device_ids=true | all-gather | bytes 16896 | tf_op jit(solution)/shard_map/all_gather | solution.py:266
  774.9 38.8 %all-gather.44.cloned.1.call-done = bf16[1024,1024]{1,0:T(8,128)(2,1)} async-done(((bf16[128,1024]{1,0:T(8,128)(2,1)}), bf16[1024,1024]{1,0:T(8,128)(2,1)}) %all-gather.44.cloned.1.call-update) | async-done | bytes 2097168 | tf_op jit(solution)/shard_map/all_gather | solution.py:38
  876.3 25.1 %reduce-scatter.82.cloned.1.call-done = f32[2,64,1024]{2,1,0:T(8,128)} async-done(((f32[2,256,1024]{2,1,0:T(8,128)}), f32[2,64,1024]{2,1,0:T(8,128)}) %reduce-scatter.82.cloned.1.call-update) | async-done | bytes 524304 | tf_op jit(solution)/shard_map/reduce_scatter | solution.py:47
  903.2 32.7 %reduce-scatter.74.cloned.1.call-done = f32[2,64,1024]{2,1,0:T(8,128)} async-done(((f32[2,256,1024]{2,1,0:T(8,128)}), f32[2,64,1024]{2,1,0:T(8,128)}) %reduce-scatter.74.cloned.1.call-update) | async-done | bytes 524304 | tf_op jit(solution)/shard_map/reduce_scatter | solution.py:47
  935.9 34.0 %reduce-scatter.66.cloned.1.call-done = f32[2,64,1024]{2,1,0:T(8,128)} async-done(((f32[2,256,1024]{2,1,0:T(8,128)}), f32[2,64,1024]{2,1,0:T(8,128)}) %reduce-scatter.66.cloned.1.call-update) | async-done | bytes 524304 | tf_op jit(solution)/shard_map/reduce_scatter | solution.py:47
  969.9 34.1 %reduce-scatter.58.cloned.1.call-done = f32[2,64,1024]{2,1,0:T(8,128)} async-done(((f32[2,256,1024]{2,1,0:T(8,128)}), f32[2,64,1024]{2,1,0:T(8,128)}) %reduce-scatter.58.cloned.1.call-update) | async-done | bytes 524304 | tf_op jit(solution)/shard_map/reduce_scatter | solution.py:47
  1168.9 28.2 %reduce-scatter.68.cloned.1.call-done = bf16[2,256,256]{2,1,0:T(8,128)(2,1)} async-done(((bf16[2,1024,256]{2,1,0:T(8,128)(2,1)}), bf16[2,256,256]{2,1,0:T(8,128)(2,1)}) %reduce-scatter.68.cloned.1.call-update) | async-done | bytes 262160 | tf_op jit(solution)/shard_map/reduce_scatter | solution.py:184
  1225.3 28.2 %reduce-scatter.60.cloned.1.call-done = bf16[2,256,256]{2,1,0:T(8,128)(2,1)} async-done(((bf16[2,1024,256]{2,1,0:T(8,128)(2,1)}), bf16[2,256,256]{2,1,0:T(8,128)(2,1)}) %reduce-scatter.60.cloned.1.call-update) | async-done | bytes 262160 | tf_op jit(solution)/shard_map/reduce_scatter | solution.py:184
  1281.5 28.2 %reduce-scatter.76.cloned.1.call-done = bf16[2,256,256]{2,1,0:T(8,128)(2,1)} async-done(((bf16[2,1024,256]{2,1,0:T(8,128)(2,1)}), bf16[2,256,256]{2,1,0:T(8,128)(2,1)}) %reduce-scatter.76.cloned.1.call-update) | async-done | bytes 262160 | tf_op jit(solution)/shard_map/reduce_scatter | solution.py:184
  1313.8 29.0 %reduce-scatter.88.cloned.1.call-done = f32[2,64,1024]{2,1,0:T(8,128)} async-done(((f32[2,256,1024]{2,1,0:T(8,128)}), f32[2,64,1024]{2,1,0:T(8,128)}) %reduce-scatter.88.cloned.1.call-update) | async-done | bytes 524304 | tf_op jit(solution)/shard_map/reduce_scatter | solution.py:47
  1342.7 34.5 %reduce-scatter.72.cloned.1.call-done = f32[2,64,1024]{2,1,0:T(8,128)} async-done(((f32[2,256,1024]{2,1,0:T(8,128)}), f32[2,64,1024]{2,1,0:T(8,128)}) %reduce-scatter.72.cloned.1.call-update) | async-done | bytes 524304 | tf_op jit(solution)/shard_map/reduce_scatter | solution.py:47
  1377.3 33.9 %reduce-scatter.64.cloned.1.call-done = f32[2,64,1024]{2,1,0:T(8,128)} async-done(((f32[2,256,1024]{2,1,0:T(8,128)}), f32[2,64,1024]{2,1,0:T(8,128)}) %reduce-scatter.64.cloned.1.call-update) | async-done | bytes 524304 | tf_op jit(solution)/shard_map/reduce_scatter | solution.py:47
  1411.1 34.0 %reduce-scatter.80.cloned.1.call-done = f32[2,64,1024]{2,1,0:T(8,128)} async-done(((f32[2,256,1024]{2,1,0:T(8,128)}), f32[2,64,1024]{2,1,0:T(8,128)}) %reduce-scatter.80.cloned.1.call-update) | async-done | bytes 524304 | tf_op jit(solution)/shard_map/reduce_scatter | solution.py:47
  1565.1 40.3 %all-reduce.15 = (f32[1024]{0:T(1024)S(1)}, f32[1024]{0:T(1024)S(1)}, f32[1024]{0:T(1024)S(1)}, f32[1024]{0:T(1024)S(1)}, f32[1024]{0:T(1024)S(1)}, /*index=5*/f...) all-reduce(f32[1024]{0:T(1024)S(1)} %dynamic-update-slice.9, ...), channel_id=1, replica_groups=mesh['fsdp'=2,'ctx'=4,'tp'=4] {'fsdp','ctx','tp'}, use_global_device_ids=true, to_apply=%add.6 | all-reduce | flops 12288 | bytes 98304
  1626.2 34.2 %reduce-scatter.56.cloned.1.call-done = f32[2,64,1024]{2,1,0:T(8,128)} async-done(((f32[2,256,1024]{2,1,0:T(8,128)}), f32[2,64,1024]{2,1,0:T(8,128)}) %reduce-scatter.56.cloned.1.call-update) | async-done | bytes 524304 | tf_op jit(solution)/shard_map/reduce_scatter | solution.py:47
  1671.8 60.0 %reduce-scatter.90.cloned.1.call-done = f32[128,2,256]{2,0,1:T(8,128)} async-done(((f32[1024,2,256]{2,0,1:T(8,128)}), f32[128,2,256]{2,0,1:T(8,128)}) %reduce-scatter.90.cloned.1.call-update) | async-done | bytes 262160 | tf_op jit(solution)/shard_map/reduce_scatter | solution.py:52
  1733.6 64.5 %reduce-scatter.94.cloned.1.call-done = f32[128,256]{1,0:T(8,128)} async-done(((f32[1024,256]{1,0:T(8,128)}), f32[128,256]{1,0:T(8,128)}) %reduce-scatter.94.cloned.1.call-update) | async-done | bytes 131088 | tf_op jit(solution)/shard_map/reduce_scatter | solution.py:54
  1798.1 91.4 %reduce-scatter.96.cloned.1.call-done = f32[128,1024]{1,0:T(8,128)} async-done(((f32[1024,1024]{1,0:T(8,128)}), f32[128,1024]{1,0:T(8,128)}) %reduce-scatter.96.cloned.1.call-update) | async-done | bytes 524304 | tf_op jit(solution)/shard_map/reduce_scatter | solution.py:55
  1889.5 91.9 %reduce-scatter.98.cloned.1.call-done = f32[128,1024]{1,0:T(8,128)} async-done(((f32[1024,1024]{1,0:T(8,128)}), f32[128,1024]{1,0:T(8,128)}) %reduce-scatter.98.cloned.1.call-update) | async-done | bytes 524304 | tf_op jit(solution)/shard_map/reduce_scatter | solution.py:56
  1981.4 79.4 %reduce-scatter.92.cloned.1.call-done = f32[128,3,256]{2,0,1:T(8,128)} async-done(((f32[1024,3,256]{2,0,1:T(8,128)}), f32[128,3,256]{2,0,1:T(8,128)}) %reduce-scatter.92.cloned.1.call-update) | async-done | bytes 393232 | tf_op jit(solution)/shard_map/reduce_scatter | solution.py:53
  (809 shorter events, 754.6 us)
Async XLA Ops:
  63.6 174.3 %all-gather.38.cloned.1.call-start = ((), (), s32[]{:S(2)}) async-start(), calls=%async_computation.36 | async-start | bytes 1769472 | tf_op jit(solution)/shard_map/all_gather | solution.py:35
  64.5 190.5 %all-gather.46.cloned.1.call-start = ((), (), s32[]{:S(2)}) async-start(), calls=%async_computation.43 | async-start | bytes 1310720 | tf_op jit(solution)/shard_map/all_gather | solution.py:43
  196.6 175.8 %all-gather.84.cloned.1.call-start = ((), (), s32[]{:S(2)}) async-start(), calls=%async_computation.91 | async-start | bytes 1310720 | tf_op jit(solution)/shard_map/all_gather | solution.py:91
  258.6 182.3 %all-gather.86.cloned.1.call-start = ((), (), s32[]{:S(2)}) async-start(), calls=%async_computation.92 | async-start | bytes 1310720 | tf_op jit(solution)/shard_map/all_gather | solution.py:91
  277.6 220.3 %all-gather.88.cloned.1.call-start = ((), (), s32[]{:S(2)}) async-start(), calls=%async_computation.93 | async-start | bytes 1310720 | tf_op jit(solution)/shard_map/all_gather | solution.py:91
  296.4 246.8 %all-gather.82.cloned.1.call-start = ((), (), s32[]{:S(2)}) async-start(), calls=%async_computation.90 | async-start | bytes 1310720 | tf_op jit(solution)/shard_map/all_gather | solution.py:91
  340.2 211.1 %reduce-scatter.42.cloned.1.call-start = ((), (), s32[]{:S(2)}) async-start(), calls=%async_computation.44 | async-start | bytes 2621440 | tf_op jit(solution)/shard_map/reduce_scatter | solution.py:47
  379.6 171.7 %reduce-scatter.48.cloned.1.call-start = ((), (), s32[]{:S(2)}) async-start(), calls=%async_computation.49 | async-start | bytes 2621440 | tf_op jit(solution)/shard_map/reduce_scatter | solution.py:47
  628.7 185.0 %all-gather.44.cloned.1.call-start = ((), (), s32[]{:S(2)}) async-start(), calls=%async_computation.40 | async-start | bytes 2359296 | tf_op jit(solution)/shard_map/all_gather | solution.py:38
  629.4 200.9 %all-gather.70.cloned.1.call-start = ((), (), s32[]{:S(2)}) async-start(), calls=%async_computation.71 | async-start | bytes 1310720 | tf_op jit(solution)/shard_map/all_gather | solution.py:43
  630.0 218.5 %all-gather.64.cloned.1.call-start = ((), (), s32[]{:S(2)}) async-start(), calls=%async_computation.64 | async-start | bytes 1310720 | tf_op jit(solution)/shard_map/all_gather | solution.py:43
  630.6 236.2 %all-gather.58.cloned.1.call-start = ((), (), s32[]{:S(2)}) async-start(), calls=%async_computation.57 | async-start | bytes 1310720 | tf_op jit(solution)/shard_map/all_gather | solution.py:43
  631.3 270.0 %reduce-scatter.82.cloned.1.call-start = ((), (), s32[]{:S(2)}) async-start(), calls=%async_computation.79 | async-start | bytes 2621440 | tf_op jit(solution)/shard_map/reduce_scatter | solution.py:47
  876.3 150.6 %all-gather.78.cloned.1.call-start = ((), (), s32[]{:S(2)}) async-start(), calls=%async_computation.80 | async-start | bytes 1310720 | tf_op jit(solution)/shard_map/all_gather | solution.py:43
  1069.8 155.4 %reduce-scatter.62.cloned.1.call-start = ((), (), s32[]{:S(2)}) async-start(), calls=%async_computation.61 | async-start | bytes 1310720 | tf_op jit(solution)/shard_map/reduce_scatter | solution.py:190
  1078.2 175.3 %reduce-scatter.60.cloned.1.call-start = ((), (), s32[]{:S(2)}) async-start(), calls=%async_computation.60 | async-start | bytes 1310720 | tf_op jit(solution)/shard_map/reduce_scatter | solution.py:184
  1091.1 190.4 %reduce-scatter.78.cloned.1.call-start = ((), (), s32[]{:S(2)}) async-start(), calls=%async_computation.75 | async-start | bytes 1310720 | tf_op jit(solution)/shard_map/reduce_scatter | solution.py:190
  1099.4 210.3 %reduce-scatter.76.cloned.1.call-start = ((), (), s32[]{:S(2)}) async-start(), calls=%async_computation.74 | async-start | bytes 1310720 | tf_op jit(solution)/shard_map/reduce_scatter | solution.py:184
  1112.4 230.3 %reduce-scatter.88.cloned.1.call-start = ((), (), s32[]{:S(2)}) async-start(), calls=%async_computation.83 | async-start | bytes 2621440 | tf_op jit(solution)/shard_map/reduce_scatter | solution.py:47
  1144.8 232.4 %reduce-scatter.72.cloned.1.call-start = ((), (), s32[]{:S(2)}) async-start(), calls=%async_computation.69 | async-start | bytes 2621440 | tf_op jit(solution)/shard_map/reduce_scatter | solution.py:47
  1200.5 210.6 %reduce-scatter.64.cloned.1.call-start = ((), (), s32[]{:S(2)}) async-start(), calls=%async_computation.62 | async-start | bytes 2621440 | tf_op jit(solution)/shard_map/reduce_scatter | solution.py:47
  1257.4 187.7 %reduce-scatter.80.cloned.1.call-start = ((), (), s32[]{:S(2)}) async-start(), calls=%async_computation.76 | async-start | bytes 2621440 | tf_op jit(solution)/shard_map/reduce_scatter | solution.py:47
  1313.7 158.0 %all-gather.74.cloned.1.call-start = ((), (), s32[]{:S(2)}) async-start(), calls=%async_computation.77 | async-start | bytes 1310720 | tf_op jit(solution)/shard_map/all_gather | solution.py:43
  1455.6 154.5 %reduce-scatter.38.cloned.1.call-start = ((), (), s32[]{:S(2)}) async-start(), calls=%async_computation.41 | async-start | bytes 2621440 | tf_op jit(solution)/shard_map/reduce_scatter | solution.py:47
  1460.2 149.9 %reduce-scatter.44.cloned.1.call-start = ((), (), s32[]{:S(2)}) async-start(), calls=%async_computation.46 | async-start | bytes 2621440 | tf_op jit(solution)/shard_map/reduce_scatter | solution.py:47
  1464.0 162.2 %reduce-scatter.50.cloned.1.call-start = ((), (), s32[]{:S(2)}) async-start(), calls=%async_computation.51 | async-start | bytes 2621440 | tf_op jit(solution)/shard_map/reduce_scatter | solution.py:47
  1467.8 192.5 %reduce-scatter.56.cloned.1.call-start = ((), (), s32[]{:S(2)}) async-start(), calls=%async_computation.56 | async-start | bytes 2621440 | tf_op jit(solution)/shard_map/reduce_scatter | solution.py:47
  1471.7 260.1 %reduce-scatter.90.cloned.1.call-start = ((), (), s32[]{:S(2)}) async-start(), calls=%async_computation.85 | async-start | bytes 2359296 | tf_op jit(solution)/shard_map/reduce_scatter | solution.py:52
  1528.3 269.8 %reduce-scatter.94.cloned.1.call-start = ((), (), s32[]{:S(2)}) async-start(), calls=%async_computation.87 | async-start | bytes 1179648 | tf_op jit(solution)/shard_map/reduce_scatter | solution.py:54
  1534.7 354.8 %reduce-scatter.96.cloned.1.call-start = ((), (), s32[]{:S(2)}) async-start(), calls=%async_computation.88 | async-start | bytes 4718592 | tf_op jit(solution)/shard_map/reduce_scatter | solution.py:55
  1544.2 437.2 %reduce-scatter.98.cloned.1.call-start = ((), (), s32[]{:S(2)}) async-start(), calls=%async_computation.89 | async-start | bytes 4718592 | tf_op jit(solution)/shard_map/reduce_scatter | solution.py:56
  1554.7 506.2 %reduce-scatter.92.cloned.1.call-start = ((), (), s32[]{:S(2)}) async-start(), calls=%async_computation.86 | async-start | bytes 3538944 | tf_op jit(solution)/shard_map/reduce_scatter | solution.py:53
  (244 other events, 11291.8 us)
Sparse Core Ops, SparseCore 0:
  10.7 42.8 all-gather.33
  57.1 30.3 reduce-scatter.33
  90.8 31.4 reduce-scatter.39
  124.7 31.3 reduce-scatter.45
  158.6 31.4 reduce-scatter.51
  192.6 45.3 all-gather.37
  313.7 47.3 all-gather.83
  362.5 33.3 all-gather.85
  397.5 37.4 all-gather.87
  436.3 48.4 all-gather.81
  519.1 31.4 reduce-scatter.47
  553.0 31.4 reduce-scatter.53
  587.0 31.3 reduce-scatter.35
  620.5 49.4 all-gather.41
  764.3 49.2 all-gather.43
  869.9 31.4 reduce-scatter.81
  904.5 31.3 reduce-scatter.73
  938.5 31.4 reduce-scatter.65
  972.6 31.3 reduce-scatter.57
  1312.6 30.0 reduce-scatter.87
  1345.8 31.3 reduce-scatter.71
  1379.6 31.4 reduce-scatter.63
  1413.7 31.3 reduce-scatter.79
  1526.0 31.4 reduce-scatter.37
  1560.7 31.5 reduce-scatter.43
  1594.8 31.3 reduce-scatter.49
  1628.9 31.4 reduce-scatter.55
  1663.9 67.8 reduce-scatter.89
  1735.6 62.4 reduce-scatter.93
  1802.6 86.8 reduce-scatter.95
  1893.8 87.6 reduce-scatter.97
  1986.1 74.7 reduce-scatter.91
  (29 shorter events, 563.9 us)
